TPU v7x, 128 devices: a whole 4x4x4 slice. The times are simulated.
128 devices in a mesh: req: 8 (over x, core), tok: 16 (over y, z).
Axes of the slice: x: 4, y: 4, z: 4, core: 2. Of those that a mesh axis runs over, the one named last changes fastest.
Arguments:
- hidden_in: bfloat16 [8, 2048, 2048], P('req', 'tok'), may hold values from -6 to 6
- attention_gain: bfloat16 [2048], replicated, may hold values from 0.25 to 1.75
- attend_matrix: bfloat16 [2048, 2560], P(None, 'req'), may hold values from -0.125 to 0.125
- merge_matrix: bfloat16 [2048, 2048], P('req'), may hold values from -1 to 1
- feedforward_gain: bfloat16 [2048], replicated, may hold values from 0.25 to 1.75
- gate_matrix: bfloat16 [2048, 8192], P(None, 'tok'), may hold values from -0.125 to 0.125
- up_matrix: bfloat16 [2048, 8192], P(None, 'tok'), may hold values from -0.125 to 0.125
- down_matrix: bfloat16 [8192, 2048], P('tok'), may hold values from -0.0625 to 0.0625
- kv_pool: bfloat16 [8, 48, 2, 128, 256], P('req', 'tok'), may hold values from -320 to 320
- lengths: int32 [8], P('req'), may hold values from 0 to 16384, as said below
- page_table: int32 [8, 16], P('req'), may hold values from 0 to 47, as said below
- free_slots: int32 [8, 16], P('req'), may hold values from 0 to 47, as said below
Outputs:
- layer_output: bfloat16 [8, 2048, 2048], P('req', 'tok')
- updated_pool: bfloat16 [8, 48, 2, 128, 256], P('req', 'tok')
Inputs may be any that keep to these rules, and one draw needn't show every extreme that they name: `lengths`: multiples of 128; in every draw some request has 0 and some has 16384. For each request the entries of its page_table row and of its free_slots row are all distinct slots of its pool. `free_slots`: see page_table.
All inputs are finite; a program needn't handle non-finite values.
Results may differ from a plain program's by a relative error of at most 0.018.
The roundings to bfloat16 on the way count: a program that leaves them out, or rounds other values in their place, can miss the bound.
Values may be sent and summed in bfloat16 or wider, within the bound.
A program may use at most 192 MiB of HBM per device.

v0:
```python
import math
import jax
import jax.numpy as jnp
from jax import lax
from jax.sharding import PartitionSpec as P

HEADS = 32
KV_HEADS = 4
HEAD_DIM = 64
WINDOW = 2048
PAGE = 128
SPAN = 2048
epsilon = 1e-05
rope_base = 10000.0


def rms_scale(matrix, gain):
    values = matrix.astype(jnp.float32)
    inverse = lax.rsqrt(jnp.mean(values * values, axis=-1, keepdims=True) + epsilon)
    return (values * inverse * gain.astype(jnp.float32)).astype(jnp.bfloat16)


def rotate(values, positions):
    half_dim = values.shape[-1] // 2
    frequency = rope_base ** (-2.0 * jnp.arange(half_dim, dtype=jnp.float32) / values.shape[-1])
    angles = positions.astype(jnp.float32)[:, None] * frequency[None, :]
    cosine = jnp.cos(angles)[:, None, :]
    sine_part = jnp.sin(angles)[:, None, :]
    lower_half = values[..., :half_dim]
    upper_half = values[..., half_dim:]
    return jnp.concatenate(
        [
            lower_half * cosine - upper_half * sine_part,
            upper_half * cosine + lower_half * sine_part,
        ],
        axis=-1,
    )


def attend(queries, all_keys, all_values, query_pos, key_pos):
    row_count = queries.shape[0]
    group_size = HEADS // KV_HEADS
    allowed = (
        (key_pos[None, :] >= 0)
        & (key_pos[None, :] <= query_pos[:, None])
        & (key_pos[None, :] > query_pos[:, None] - WINDOW)
    )
    factor = 1.0 / math.sqrt(HEAD_DIM)
    blocks = []
    for head_index in range(KV_HEADS):
        query_block = queries[
            :, head_index * group_size * HEAD_DIM : (head_index + 1) * group_size * HEAD_DIM
        ].reshape(row_count * group_size, HEAD_DIM)
        key_block = all_keys[:, head_index * HEAD_DIM : (head_index + 1) * HEAD_DIM]
        value_block = all_values[:, head_index * HEAD_DIM : (head_index + 1) * HEAD_DIM]
        scores = (
            lax.dot_general(
                query_block, key_block, (((1,), (1,)), ((), ())), preferred_element_type=jnp.float32
            )
            * factor
        )
        scores = jnp.where(allowed[:, None, :], scores.reshape(row_count, group_size, -1), -jnp.inf)
        row_peak = jnp.max(scores, axis=-1, keepdims=True)
        weights = jnp.exp(scores - row_peak)
        row_total = jnp.sum(weights, axis=-1, keepdims=True)
        weighted = jnp.dot(
            weights.astype(jnp.bfloat16).reshape(row_count * group_size, -1),
            value_block,
            preferred_element_type=jnp.float32,
        )
        blocks.append(weighted.reshape(row_count, group_size, HEAD_DIM) / row_total)
    return jnp.concatenate(blocks, axis=1).reshape(row_count, HEADS * HEAD_DIM).astype(jnp.bfloat16)


def shards(
    hidden_in,
    attention_gain,
    attend_matrix,
    merge_matrix,
    feedforward_gain,
    gate_matrix,
    up_matrix,
    down_matrix,
    kv_pool,
    lengths,
    page_table,
    free_slots,
):
    tokens = hidden_in[0]
    tok_rows = tokens.shape[0]
    length = lengths[0]
    tok_index = lax.axis_index("tok")
    query_width = HEADS * HEAD_DIM
    kv_width = KV_HEADS * HEAD_DIM
    normed = rms_scale(tokens, attention_gain)
    projected = jnp.dot(
        normed,
        lax.all_gather(attend_matrix, "req", axis=1, tiled=True),
        preferred_element_type=jnp.float32,
    )
    positions = length + tok_index * tok_rows + jnp.arange(tok_rows, dtype=jnp.int32)
    queries = (
        rotate(projected[:, :query_width].reshape(tok_rows, HEADS, HEAD_DIM), positions)
        .astype(jnp.bfloat16)
        .reshape(tok_rows, query_width)
    )
    new_keys = (
        rotate(
            projected[:, query_width : query_width + kv_width].reshape(
                tok_rows, KV_HEADS, HEAD_DIM
            ),
            positions,
        )
        .astype(jnp.bfloat16)
        .reshape(tok_rows, kv_width)
    )
    new_values = projected[:, query_width + kv_width :].astype(jnp.bfloat16)
    fresh = jnp.stack([new_keys, new_values])
    table = page_table[0]
    pool_local = kv_pool[0]
    slot_count = pool_local.shape[0]
    key_pos = jnp.concatenate(
        [
            length - WINDOW + jnp.arange(WINDOW, dtype=jnp.int32),
            length + jnp.arange(SPAN, dtype=jnp.int32),
        ]
    )
    whole_pool, span_kv = (
        lax.all_gather(pool_local, "tok", axis=0, tiled=True),
        lax.all_gather(fresh, "tok", axis=1, tiled=True),
    )
    window_pages = whole_pool[table]
    window = jnp.transpose(window_pages, (1, 0, 2, 3)).reshape(2, WINDOW, kv_width)
    all_keys = jnp.concatenate([window[0], span_kv[0]], axis=0)
    all_values = jnp.concatenate([window[1], span_kv[1]], axis=0)
    attended = attend(queries, all_keys, all_values, positions, key_pos)
    merged = jnp.dot(
        attended,
        lax.all_gather(merge_matrix, "req", axis=0, tiled=True),
        preferred_element_type=jnp.float32,
    )
    residual = (tokens.astype(jnp.float32) + merged).astype(jnp.bfloat16)
    normed_two = rms_scale(residual, feedforward_gain)
    piece = lax.all_gather(normed_two, "tok", axis=0, tiled=True)
    gate = jnp.dot(piece, gate_matrix, preferred_element_type=jnp.float32)
    lifted = jnp.dot(piece, up_matrix, preferred_element_type=jnp.float32)
    inner = (jax.nn.silu(gate) * lifted).astype(jnp.bfloat16)
    feed_sum = lax.psum_scatter(
        jnp.dot(inner, down_matrix, preferred_element_type=jnp.float32).astype(jnp.bfloat16),
        "tok",
        scatter_dimension=0,
        tiled=True,
    ).astype(jnp.float32)
    output_rows = (residual.astype(jnp.float32) + feed_sum).astype(jnp.bfloat16)
    span_pages = jnp.transpose(span_kv.reshape(2, -1, PAGE, kv_width), (1, 0, 2, 3)).reshape(
        -1, 2 * PAGE * kv_width
    )
    slot_ids = tok_index * slot_count + jnp.arange(slot_count, dtype=jnp.int32)
    hits = free_slots[0][:, None] == slot_ids[None, :]
    placed = jnp.dot(
        hits.T.astype(jnp.bfloat16), span_pages, preferred_element_type=jnp.float32
    ).astype(jnp.bfloat16)
    filled = jnp.any(hits, axis=0)
    new_local = jnp.where(filled[:, None], placed, pool_local.reshape(slot_count, -1)).reshape(
        pool_local.shape
    )
    return (output_rows[None], new_local[None])


def solution(mesh):
    in_specs = (
        P("req", "tok", None),
        P(),
        P(None, "req"),
        P("req", None),
        P(),
        P(None, "tok"),
        P(None, "tok"),
        P("tok", None),
        P("req", "tok", None, None, None),
        P("req"),
        P("req", None),
        P("req", None),
    )
    out_specs = (P("req", "tok", None), P("req", "tok", None, None, None))
    return jax.shard_map(shards, mesh=mesh, in_specs=in_specs, out_specs=out_specs, check_vma=False)
```

profile of v0, /device:TPU:0, one launch (start us, length us, event | category | flops | bytes accessed | tf_op | source)
XLA Modules:
  0.0 495.1 jit_solution(5422393947155966126)
XLA Ops:
  7.2 0.7 all-gather.7.cloned.1.call-update
  8.0 0.7 all-gather.15.cloned.1.call-update
  8.7 0.7 convert_element_type.89
  10.1 1.2 fusion.31
  11.3 0.7 multiply_cosine_fusion
  12.1 58.5 %all-gather.7.cloned.1.call-done = bf16[2048,2560]{0,1:T(8,128)(2,1)} async-done(((bf16[2048,320]{0,1:T(8,128)(2,1)}), bf16[2048,2560]{0,1:T(8,128)(2,1)}) %all-gather.7.cloned.1.call-update) | async-done | bytes 10485776 | tf_op jit(solution)/shard_map/all_gather | solution.py:98
  70.6 7.8 %fusion.98 = f32[128,2560]{1,0:T(8,128)S(1)} fusion(bf16[2048,2560]{0,1:T(8,128)(2,1)} %all-gather.7.cloned.1.call-done, bf16[1,128,2048]{2,1,0:T(8,128)(2,1)} %param.12, f32[2048]{0:T(1024)S(1)} %convert_element_type.89, f32[128]{0:T(128)S(1)} %add_rsqrt_fusion.1), kind=kOutput, calls=%fused_computation.91 | convolution fusion | flops 1343225856 | bytes 12329472 | tf_op jit(solution)/shard_map/dot_general | solution.py:96
  78.4 0.7 slice.102
  79.1 1.0 copy.72
  80.1 0.7 subtract_convert_fusion.1
  80.9 0.1 copy.73
  81.0 0.7 pad_maximum_fusion.5
  81.8 0.5 all-gather.11.cloned.1.call-update
  82.4 0.7 fusion.107
  83.1 1.3 convert_element_type.101
  84.3 1.4 compare_and_fusion
  85.8 48.8 %all-gather.15.cloned.1.call-done = bf16[1,48,2,128,256]{4,3,2,0,1:T(8,128)(2,1)} async-done(((bf16[1,3,2,128,256]{4,3,2,0,1:T(8,128)(2,1)}), bf16[1,48,2,128,256]{4,3,2,0,1:T(8,128)(2,1)}) %all-gather.15.cloned.1.call-update) | async-done | bytes 6291472 | tf_op jit(solution)/shard_map/all_gather | solution.py:129
  134.6 4.8 gather_fusion
  139.4 2.7 fusion.126
  142.1 2.3 slice.97
  144.4 2.6 copy.69
  147.0 1.3 subtract_convert_fusion
  148.3 0.1 pad_maximum_fusion.4
  148.4 0.8 fusion.127
  149.1 0.1 copy.70
  149.3 0.2 reshape.306
  149.4 1.0 copy.77
  150.5 0.9 reshape.309
  151.4 1.0 copy.75
  152.4 0.9 reshape.308
  153.3 1.0 copy.79
  154.3 0.9 reshape.310
  155.2 26.3 %all-gather.9.cloned.1.call-done = bf16[2,2048,256]{2,1,0:T(8,128)(2,1)} async-done(((bf16[2,128,256]{2,1,0:T(8,128)(2,1)}), bf16[2,2048,256]{2,1,0:T(8,128)(2,1)}) %all-gather.9.cloned.1.call-update) | async-done | bytes 2097168 | tf_op jit(solution)/shard_map/all_gather | solution.py:130
  181.5 2.7 slice_bitcast_fusion.1
  184.2 10.5 %fusion.44 = f32[1024,4096]{1,0:T(8,128)} fusion(bf16[1024,64]{1,0:T(8,128)(2,1)} %reshape.309, bf16[2048,256]{1,0:T(8,128)(2,1)S(1)} %bitcast.173, bf16[2048,256]{1,0:T(8,128)(2,1)S(1)} %get-tuple-element.11), kind=kOutput, calls=%fused_computation.65 | convolution fusion | flops 537919488 | bytes 19005440 | tf_op jit(solution)/shard_map/dot_general | solution.py:57
  194.6 8.1 %fusion.50 = f32[1024,4096]{1,0:T(8,128)} fusion(bf16[1024,64]{1,0:T(8,128)(2,1)S(1)} %copy-done.7, bf16[2048,256]{1,0:T(8,128)(2,1)S(1)} %bitcast.174, bf16[2048,256]{1,0:T(8,128)(2,1)S(1)} %get-tuple-element.11), kind=kOutput, calls=%fused_computation.69 | convolution fusion | flops 537919488 | bytes 19005440 | tf_op jit(solution)/shard_map/dot_general | solution.py:57
  202.8 9.0 %fusion.9 = (f32[1024]{0:T(1024)S(1)}, f32[1024,4096]{1,0:T(8,128)}) fusion(pred[128,4096]{1,0:T(8,128)(4,1)S(1)} %copy-done.2, bf16[1024,64]{1,0:T(8,128)(2,1)S(1)} %reshape.306, bf16[2048,256]{1,0:T(8,128)(2,1)S(1)} %bitcast.175, bf16[2048,256]{1,0:T(8,128)(2,1)S(1)} %get-tuple-element.11), kind=kOutput, calls=%fused_computation.19 | convolution fusion | flops 550501376 | bytes 19533824 | tf_op jit(solution)/shard_map/dot_general | solution.py:57
  211.7 28.7 %fusion.1 = (f32[1024]{0:T(1024)S(1)}, f32[1024]{0:T(1024)S(1)}, f32[1024]{0:T(1024)S(1)}, f32[1024]{0:T(1024)S(1)}, f32[1024,4096]{1,0:T(8,128)}) fusion(f32[1024,4096]{1,0:T(8,128)} %get-tuple-element.24, f32[1024]{0:T(1024)S(1)} %get-tuple-element.23, pred[128,4096]{1,0:T(8,128)(4,1)} %compare_and_fusion, f32[1024,4096]{1,0:T(8,128)} %fusion.44, ...), kind=kOutput, calls=%fused_computation.11 | convolution fusion | flops 592441344 | bytes 69881856 | tf_op jit(solution)/shard_map/dot_general | solution.py:57
  240.4 20.7 %fusion.3 = (f32[1024]{0:T(1024)S(1)}, f32[1024]{0:T(1024)S(1)}, f32[1024]{0:T(1024)S(1)}) fusion(f32[1024,4096]{1,0:T(8,128)} %fusion.50, f32[1024]{0:T(1024)S(1)} %get-tuple-element.5, pred[128,4096]{1,0:T(8,128)(4,1)} %compare_and_fusion, f32[1024]{0:T(1024)S(1)} %get-tuple-element.4, f32[1024,4096]{1,0:T(8,128)} %fusion.44, ...), kind=kLoop, calls=%fused_computation.13 | loop fusion | flops 50328576 | bytes 50880512 | tf_op jit(solution)/shard_map/reduce_sum | solution.py:65
  261.1 0.1 div.68
  261.2 0.7 div.65
  261.9 0.7 div.62
  262.6 0.7 div.59
  263.3 9.8 %fusion.62 = bf16[128,8,64]{2,1,0:T(8,128)(2,1)} fusion(bf16[2048,256]{1,0:T(8,128)(2,1)} %get-tuple-element.12, bf16[2048,256]{1,0:T(8,128)(2,1)} %bitcast.186, f32[1024,4096]{1,0:T(8,128)} %get-tuple-element.25, f32[1024]{0:T(1024)S(1)} %get-tuple-element.3, pred[128,4096]{1,0:T(8,128)(4,1)S(1)} %copy-done.3, f32[128,8]{1,0:T(8,128)S(1)} %div.68), kind=kOutput, calls=%fused_computation.83 | convolution fusion | flops 554827776 | bytes 19537920 | tf_op jit(solution)/shard_map/dot_general | solution.py:66
  273.1 9.2 %fusion.72 = bf16[128,8,64]{2,1,0:T(8,128)(2,1)} fusion(bf16[2048,256]{1,0:T(8,128)(2,1)} %bitcast.187, bf16[2048,256]{1,0:T(8,128)(2,1)} %get-tuple-element.12, f32[1024,4096]{1,0:T(8,128)} %fusion.44, f32[1024]{0:T(1024)S(1)} %get-tuple-element.4, pred[128,4096]{1,0:T(8,128)(4,1)S(1)} %copy-done.3, f32[128,8]{1,0:T(8,128)} %div.65), kind=kOutput, calls=%fused_computation.85 | convolution fusion | flops 554827776 | bytes 19537920 | tf_op jit(solution)/shard_map/dot_general | solution.py:66
  282.3 6.5 %fusion.82 = bf16[128,8,64]{2,1,0:T(8,128)(2,1)} fusion(bf16[2048,256]{1,0:T(8,128)(2,1)} %bitcast.188, bf16[2048,256]{1,0:T(8,128)(2,1)} %get-tuple-element.12, f32[1024,4096]{1,0:T(8,128)S(1)} %bitcast.172, f32[1024]{0:T(1024)S(1)} %get-tuple-element.5, pred[128,4096]{1,0:T(8,128)(4,1)S(1)} %copy-done.3, f32[128,8]{1,0:T(8,128)} %div.62), kind=kOutput, calls=%fused_computation.87 | convolution fusion | flops 554827776 | bytes 19537920 | tf_op jit(solution)/shard_map/dot_general | solution.py:66
  288.8 8.8 %fusion.92 = bf16[128,8,64]{2,1,0:T(8,128)(2,1)S(1)} fusion(bf16[2048,256]{1,0:T(8,128)(2,1)} %bitcast.189, bf16[2048,256]{1,0:T(8,128)(2,1)} %get-tuple-element.12, f32[1024,4096]{1,0:T(8,128)} %get-tuple-element.24, f32[1024]{0:T(1024)S(1)} %get-tuple-element.23, pred[128,4096]{1,0:T(8,128)(4,1)S(1)} %copy-done.3, f32[128,8]{1,0:T(8,128)} %div.59), kind=kOutput, calls=%fused_computation.89 | convolution fusion | flops 554827776 | bytes 19537920 | tf_op jit(solution)/shard_map/dot_general | solution.py:66
  297.6 0.3 pad_maximum_fusion.3
  297.9 1.9 copy.81
  299.8 4.9 multiply_reduce_fusion
  304.7 1.0 multiply_convert_fusion.1
  305.7 0.0 reduce-scatter.2.cloned.1.call-start
  305.8 69.4 %all-gather.13.cloned.1.call-done = bf16[2048,2048]{1,0:T(8,128)(2,1)} async-done(((bf16[128,2048]{1,0:T(8,128)(2,1)}), bf16[2048,2048]{1,0:T(8,128)(2,1)}) %all-gather.13.cloned.1.call-update) | async-done | bytes 8388624 | tf_op jit(solution)/shard_map/all_gather | solution.py:144
  375.2 10.5 %fusion.128 = f32[2048,512]{1,0:T(8,128)} fusion(bf16[2048,2048]{1,0:T(8,128)(2,1)} %all-gather.13.cloned.1.call-done, bf16[2048,512]{1,0:T(8,128)(2,1)} %param.17), kind=kOutput, calls=%fused_computation.143 | convolution fusion | flops 4294967296 | bytes 14680064 | tf_op jit(solution)/shard_map/dot_general | solution.py:145
  385.7 14.8 %convolution_convert_fusion.1 = bf16[2048,2048]{1,0:T(8,128)(2,1)} fusion(bf16[512,2048]{1,0:T(8,128)(2,1)S(1)} %copy-done, f32[2048,512]{1,0:T(8,128)} %fusion.128, bf16[2048,2048]{1,0:T(8,128)(2,1)} %all-gather.13.cloned.1.call-done, bf16[2048,512]{1,0:T(8,128)(2,1)} %param.18), kind=kOutput, calls=%fused_computation.35 | convolution fusion | flops 8600420352 | bytes 25165824 | tf_op jit(solution)/shard_map/dot_general | solution.py:149
  400.5 1.0 copy-done.6
  401.5 1.0 reshape_squeeze.3
  402.4 0.2 compare_reduce_fusion
  402.6 1.7 copy.82
  404.4 1.2 copy.91
  405.6 0.7 fusion
  406.3 0.8 copy.92
  407.1 79.1 %reduce-scatter.2.cloned.1.call-done = bf16[128,2048]{1,0:T(8,128)(2,1)} async-done(((bf16[2048,2048]{1,0:T(8,128)(2,1)}), bf16[128,2048]{1,0:T(8,128)(2,1)}) %reduce-scatter.2.cloned.1.call-update) | async-done | bytes 524304 | tf_op jit(solution)/shard_map/reduce_scatter | solution.py:148
  486.2 1.9 fusion.97
  (57 shorter events, 0.4 us)
Async XLA Ops:
  7.2 378.5 %copy-start = (bf16[512,2048]{1,0:T(8,128)(2,1)S(1)}, bf16[512,2048]{1,0:T(8,128)(2,1)}, u32[]{:S(2)}) copy-start(bf16[512,2048]{1,0:T(8,128)(2,1)} %param.19) | copy-start | bytes 6291460
  7.2 63.4 %all-gather.7.cloned.1.call-start = ((), (), s32[]{:S(2)}) async-start(), calls=%async_computation.1 | async-start | bytes 11796480 | tf_op jit(solution)/shard_map/all_gather | solution.py:98
  7.9 126.7 %all-gather.15.cloned.1.call-start = ((), (), s32[]{:S(2)}) async-start(), calls=%async_computation.6 | async-start | bytes 6684672 | tf_op jit(solution)/shard_map/all_gather | solution.py:129
  8.7 172.8 %all-gather.9.cloned.1.call-start = ((), (), s32[]{:S(2)}) async-start(), calls=%async_computation.2 | async-start | bytes 2228224 | tf_op jit(solution)/shard_map/all_gather | solution.py:130
  78.4 61.0 %copy-start.4 = (f32[128,2560]{1,0:T(8,128)}, f32[128,2560]{1,0:T(8,128)S(1)}, u32[]{:S(2)}) copy-start(f32[128,2560]{1,0:T(8,128)S(1)} %fusion.98) | copy-start | bytes 3932164
  81.7 65.3 %copy-start.11 = (f32[128,32]{0,1:T(8,128)S(1)}, f32[128,32]{0,1:T(8,128)}, u32[]{:S(2)}) copy-start(f32[128,32]{0,1:T(8,128)} %get-tuple-element.22) | copy-start | bytes 49156
  81.7 218.1 %all-gather.11.cloned.1.call-start = ((), (), s32[]{:S(2)}) async-start(), calls=%async_computation.3 | async-start | bytes 9437184 | tf_op jit(solution)/shard_map/all_gather | solution.py:139
  82.3 292.9 %all-gather.13.cloned.1.call-start = ((), (), s32[]{:S(2)}) async-start(), calls=%async_computation.4 | async-start | bytes 8912896 | tf_op jit(solution)/shard_map/all_gather | solution.py:144
  184.2 18.6 %copy-start.1 = (bf16[2048,256]{1,0:T(8,128)(2,1)}, bf16[2048,256]{1,0:T(8,128)(2,1)S(1)}, u32[]{:S(2)}) copy-start(bf16[2048,256]{1,0:T(8,128)(2,1)S(1)} %get-tuple-element.11) | copy-start | bytes 3145732
  184.2 10.5 %copy-start.7 = (bf16[1024,64]{1,0:T(8,128)(2,1)S(1)}, bf16[1024,64]{1,0:T(8,128)(2,1)}, u32[]{:S(2)}) copy-start(bf16[1024,64]{1,0:T(8,128)(2,1)} %reshape.308) | copy-start | bytes 393220
  194.6 8.1 %copy-start.2 = (pred[128,4096]{1,0:T(8,128)(4,1)S(1)}, pred[128,4096]{1,0:T(8,128)(4,1)}, u32[]{:S(2)}) copy-start(pred[128,4096]{1,0:T(8,128)(4,1)} %compare_and_fusion) | copy-start | bytes 1572868
  240.4 22.9 %copy-start.3 = (pred[128,4096]{1,0:T(8,128)(4,1)S(1)}, pred[128,4096]{1,0:T(8,128)(4,1)}, u32[]{:S(2)}) copy-start(pred[128,4096]{1,0:T(8,128)(4,1)} %compare_and_fusion) | copy-start | bytes 1572868
  263.3 19.0 %slice-start = ((s8[16777216]{0:T(1024)(128)(4,1)}), s8[4194304]{0:T(1024)(128)(4,1)S(1)}, s32[]{:S(2)}) async-start(s8[16777216]{0:T(1024)(128)(4,1)} %bitcast.171), calls=%async_computation.7 | async-start | bytes 8388608
  263.3 19.0 %slice-start.1 = ((s8[16777216]{0:T(1024)(128)(4,1)}), s8[4194304]{0:T(1024)(128)(4,1)S(1)}, s32[]{:S(2)}) async-start(s8[16777216]{0:T(1024)(128)(4,1)} %bitcast.171), calls=%async_computation.8 | async-start | bytes 8388608
  273.1 9.2 %slice-start.2 = ((s8[16777216]{0:T(1024)(128)(4,1)}), s8[4194304]{0:T(1024)(128)(4,1)S(1)}, s32[]{:S(2)}) async-start(s8[16777216]{0:T(1024)(128)(4,1)} %bitcast.171), calls=%async_computation.9 | async-start | bytes 8388608
  273.1 9.2 %slice-start.3 = ((s8[16777216]{0:T(1024)(128)(4,1)}), s8[4194304]{0:T(1024)(128)(4,1)S(1)}, s32[]{:S(2)}) async-start(s8[16777216]{0:T(1024)(128)(4,1)} %bitcast.171), calls=%async_computation.10 | async-start | bytes 8388608
  288.8 8.8 %copy-start.8 = (bf16[128,8,64]{2,1,0:T(8,128)(2,1)S(1)}, bf16[128,8,64]{2,1,0:T(8,128)(2,1)}, u32[]{:S(2)}) copy-start(bf16[128,8,64]{2,1,0:T(8,128)(2,1)} %fusion.62) | copy-start | bytes 393220
  288.8 8.8 %copy-start.9 = (bf16[128,8,64]{2,1,0:T(8,128)(2,1)S(1)}, bf16[128,8,64]{2,1,0:T(8,128)(2,1)}, u32[]{:S(2)}) copy-start(bf16[128,8,64]{2,1,0:T(8,128)(2,1)} %fusion.72) | copy-start | bytes 393220
  288.8 8.8 %copy-start.10 = (bf16[128,8,64]{2,1,0:T(8,128)(2,1)S(1)}, bf16[128,8,64]{2,1,0:T(8,128)(2,1)}, u32[]{:S(2)}) copy-start(bf16[128,8,64]{2,1,0:T(8,128)(2,1)} %fusion.82) | copy-start | bytes 393220
  299.8 5.0 %copy-start.12 = (f32[2048]{0:T(1024)S(1)}, f32[2048]{0:T(1024)}, u32[]{:S(2)}) copy-start(f32[2048]{0:T(1024)} %convert_element_type.101) | copy-start | bytes 24580
  305.7 180.4 %reduce-scatter.2.cloned.1.call-start = ((), (), s32[]{:S(2)}) async-start(), calls=%async_computation.5 | async-start | bytes 8912896 | tf_op jit(solution)/shard_map/reduce_scatter | solution.py:148
  400.5 1.0 copy-start.6
  400.5 2.0 copy-start.13
  402.4 3.1 copy-start.5
Sparse Core Ops, SparseCore 0:
  9.7 60.9 all-gather.6
  72.8 61.7 all-gather.14
  136.8 44.6 all-gather.8
  183.0 48.8 all-gather.10
  305.8 69.3 all-gather.12
  400.6 85.4 reduce-scatter.1
where the time goes:
time: 503 us; the launch traced here: 495 us
  waiting for transfers between devices  284 us (56%)
  matrix products  129 us (26%)
  local copies, waits for them, and re-layouts  33.4 us (7%)
  other arithmetic  32.9 us (7%)
  between operations  15.2 us (3%)
    reduce_scatter x1, waiting for transfers between devices, shards(): lax.psum_scatter(jnp.dot(inner, down_matrix, preferred_element_type=jnp.f...  79.1 us
    all_gather x1, waiting for transfers between devices, shards(): piece = lax.all_gather(normed_two, 'tok', axis=0, tiled=True)  69.4 us
    all_gather x1, waiting for transfers between devices, shards(): lax.all_gather(attend_matrix, 'req', axis=1, tiled=True)  58.5 us
    dot_general x4, matrix products, attend(): lax.dot_general(query_block, key_block, (((1,), (1,)), ((), ())), preferr...  56.2 us
    all_gather x1, waiting for transfers between devices, shards(): lax.all_gather(pool_local, 'tok', axis=0, tiled=True)  48.8 us
    dot_general x4, matrix products, attend(): jnp.dot(weights.astype(jnp.bfloat16).reshape(row_count * group_size, -1),...  34.2 us
    all_gather x1, waiting for transfers between devices, shards(): lax.all_gather(fresh, 'tok', axis=1, tiled=True)  26.3 us
    reduce_sum x1, other arithmetic, attend(): row_total = jnp.sum(weights, axis=-1, keepdims=True)  20.7 us
  transfers between devices with their start and end apart: 6, of which 5 were waited for; matrix products, arithmetic and copies ran while one was open for 33% of the time, Pallas kernels for 0%

commit v1 on v0

--- a/solution.py
+++ b/solution.py
@@ -12,6 +12,28 @@
 SPAN = 2048
 epsilon = 1e-05
 rope_base = 10000.0
+
+
+def joined_along(parts, dim):
+    parts = jnp.moveaxis(parts, 0, dim)
+    lengths = parts.shape
+    return parts.reshape(*lengths[:dim], lengths[dim] * lengths[dim + 1], *lengths[dim + 2 :])
+
+
+def collect(value, axis, dim):
+    size = lax.axis_size(axis)
+    pairs = [(i, (i + 1) % size) for i in range(size)]
+    back = [(b, a) for a, b in pairs]
+    lower, upper = ([], [])
+    for step in range(size - 1):
+        if step % 2 == 0:
+            lower.append(lax.ppermute(lower[-1] if lower else value, axis, pairs))
+        else:
+            upper.append(lax.ppermute(upper[-1] if upper else value, axis, back))
+    blocks = jnp.stack([*lower[::-1], value, *upper])
+    shift = lax.axis_index(axis) - len(lower)
+    blocks = blocks[(jnp.arange(size) - shift) % size]
+    return joined_along(blocks, dim)
 
 
 def rms_scale(matrix, gain):
@@ -141,7 +163,7 @@
     )
     residual = (tokens.astype(jnp.float32) + merged).astype(jnp.bfloat16)
     normed_two = rms_scale(residual, feedforward_gain)
-    piece = lax.all_gather(normed_two, "tok", axis=0, tiled=True)
+    piece = collect(normed_two, "tok", 0)
     gate = jnp.dot(piece, gate_matrix, preferred_element_type=jnp.float32)
     lifted = jnp.dot(piece, up_matrix, preferred_element_type=jnp.float32)
     inner = (jax.nn.silu(gate) * lifted).astype(jnp.bfloat16)

time: 503 us -> 576 us (1.15)
  starting transfers between devices: 0.24 us -> 40.6 us
  local copies, waits for them, and re-layouts: 33.4 us -> 67.7 us
    ppermute x0 -> x15, waiting for transfers between devices: none -> 70 us  [the longest x8 67.9 us: collect(): lower.append(lax.ppermute(lower[-1] if lower else value, axis, pairs))]
    all_gather x1 -> x0, waiting for transfers between devices: 69.4 us -> none  [shards(): piece = lax.all_gather(normed_two, 'tok', axis=0, tiled=True)]
    ppermute x0 -> x15, starting transfers between devices: none -> 40.4 us  [the longest x7 39.5 us: collect(): upper.append(lax.ppermute(upper[-1] if upper else value, axis, back))]
    unnamed x38 -> x80, local copies, waits for them, and re-layouts: 3.03 us -> 27.9 us
    gather x0 -> x1, local copies, waits for them, and re-layouts: none -> 8.34 us  [collect(): blocks = blocks[(jnp.arange(size) - shift) % size]]
  transfers between devices with their start and end apart: 6 -> 20, of which waited for: 5 -> 16; matrix products, arithmetic and copies ran while one was open for 33% -> 33% of each run, Pallas kernels for 0% -> 0%
where the time goes in v1:
time: 576 us; the launch traced here: 567 us
  waiting for transfers between devices  281 us (49%)
  matrix products  129 us (22%)
  local copies, waits for them, and re-layouts  67.7 us (12%)
  starting transfers between devices  40.6 us (7%)
  other arithmetic  33.2 us (6%)
  between operations  15 us (3%)
    reduce_scatter x1, waiting for transfers between devices, shards(): lax.psum_scatter(jnp.dot(inner, down_matrix, preferred_element_type=jnp.f...  75.8 us
    ppermute x8, waiting for transfers between devices, collect(): lower.append(lax.ppermute(lower[-1] if lower else value, axis, pairs))  67.9 us
    all_gather x1, waiting for transfers between devices, shards(): lax.all_gather(attend_matrix, 'req', axis=1, tiled=True)  58.5 us
    dot_general x4, matrix products, attend(): lax.dot_general(query_block, key_block, (((1,), (1,)), ((), ())), preferr...  56.3 us
    all_gather x1, waiting for transfers between devices, shards(): lax.all_gather(pool_local, 'tok', axis=0, tiled=True)  48.8 us
    ppermute x7, starting transfers between devices, collect(): upper.append(lax.ppermute(upper[-1] if upper else value, axis, back))  39.5 us
    dot_general x4, matrix products, attend(): jnp.dot(weights.astype(jnp.bfloat16).reshape(row_count * group_size, -1),...  34.2 us
    unnamed x80, local copies, waits for them, and re-layouts  27.9 us
  transfers between devices with their start and end apart: 20, of which 16 were waited for; matrix products, arithmetic and copies ran while one was open for 33% of the time, Pallas kernels for 0%

profile of v1, /device:TPU:0, one launch (start us, length us, event | category | flops | bytes accessed | tf_op | source)
XLA Modules:
  0.0 567.0 jit_solution(9451250121456226234)
XLA Ops:
  10.1 1.2 fusion.31
  12.1 58.5 %all-gather.6.cloned.1.call-done = bf16[2048,2560]{0,1:T(8,128)(2,1)} async-done(((bf16[2048,320]{0,1:T(8,128)(2,1)}), bf16[2048,2560]{0,1:T(8,128)(2,1)}) %all-gather.6.cloned.1.call-update) | async-done | bytes 10485776 | tf_op jit(solution)/shard_map/all_gather | solution.py:120
  70.6 7.8 %fusion.98 = f32[128,2560]{1,0:T(8,128)S(1)} fusion(bf16[2048,2560]{0,1:T(8,128)(2,1)} %all-gather.6.cloned.1.call-done, bf16[1,128,2048]{2,1,0:T(8,128)(2,1)} %param.12, f32[2048]{0:T(1024)S(1)} %convert_element_type.89, f32[128]{0:T(128)S(1)} %add_rsqrt_fusion.1), kind=kOutput, calls=%fused_computation.92 | convolution fusion | flops 1343225856 | bytes 12329472 | tf_op jit(solution)/shard_map/dot_general | solution.py:118
  79.1 1.0 copy.72
  83.0 1.3 convert_element_type.101
  84.3 1.4 compare_and_fusion
  85.8 48.8 %all-gather.12.cloned.1.call-done = bf16[1,48,2,128,256]{4,3,2,0,1:T(8,128)(2,1)} async-done(((bf16[1,3,2,128,256]{4,3,2,0,1:T(8,128)(2,1)}), bf16[1,48,2,128,256]{4,3,2,0,1:T(8,128)(2,1)}) %all-gather.12.cloned.1.call-update) | async-done | bytes 6291472 | tf_op jit(solution)/shard_map/all_gather | solution.py:151
  134.6 4.8 gather_fusion
  139.4 2.7 fusion.128
  142.1 2.3 slice.99
  144.5 2.6 copy.69
  147.0 1.3 subtract_convert_fusion
  149.5 1.0 copy.77
  151.4 1.0 copy.75
  153.3 1.0 copy.79
  155.2 26.2 %all-gather.8.cloned.1.call-done = bf16[2,2048,256]{2,1,0:T(8,128)(2,1)} async-done(((bf16[2,128,256]{2,1,0:T(8,128)(2,1)}), bf16[2,2048,256]{2,1,0:T(8,128)(2,1)}) %all-gather.8.cloned.1.call-update) | async-done | bytes 2097168 | tf_op jit(solution)/shard_map/all_gather | solution.py:152
  181.5 2.7 slice_bitcast_fusion.1
  184.2 10.5 %fusion.44 = f32[1024,4096]{1,0:T(8,128)} fusion(bf16[1024,64]{1,0:T(8,128)(2,1)} %reshape.361, bf16[2048,256]{1,0:T(8,128)(2,1)S(1)} %bitcast.208, bf16[2048,256]{1,0:T(8,128)(2,1)S(1)} %get-tuple-element.11), kind=kOutput, calls=%fused_computation.66 | convolution fusion | flops 537919488 | bytes 19005440 | tf_op jit(solution)/shard_map/dot_general | solution.py:79
  194.6 8.2 %fusion.50 = f32[1024,4096]{1,0:T(8,128)} fusion(bf16[1024,64]{1,0:T(8,128)(2,1)S(1)} %copy-done.7, bf16[2048,256]{1,0:T(8,128)(2,1)S(1)} %bitcast.209, bf16[2048,256]{1,0:T(8,128)(2,1)S(1)} %get-tuple-element.11), kind=kOutput, calls=%fused_computation.70 | convolution fusion | flops 537919488 | bytes 19005440 | tf_op jit(solution)/shard_map/dot_general | solution.py:79
  202.8 9.0 %fusion.9 = (f32[1024]{0:T(1024)S(1)}, f32[1024,4096]{1,0:T(8,128)}) fusion(pred[128,4096]{1,0:T(8,128)(4,1)S(1)} %copy-done.2, bf16[1024,64]{1,0:T(8,128)(2,1)S(1)} %reshape.358, bf16[2048,256]{1,0:T(8,128)(2,1)S(1)} %bitcast.210, bf16[2048,256]{1,0:T(8,128)(2,1)S(1)} %get-tuple-element.11), kind=kOutput, calls=%fused_computation.20 | convolution fusion | flops 550501376 | bytes 19533824 | tf_op jit(solution)/shard_map/dot_general | solution.py:79
  211.8 28.7 %fusion.1 = (f32[1024]{0:T(1024)S(1)}, f32[1024]{0:T(1024)S(1)}, f32[1024]{0:T(1024)S(1)}, f32[1024]{0:T(1024)S(1)}, f32[1024,4096]{1,0:T(8,128)}) fusion(f32[1024,4096]{1,0:T(8,128)} %get-tuple-element.24, f32[1024]{0:T(1024)S(1)} %get-tuple-element.23, pred[128,4096]{1,0:T(8,128)(4,1)} %compare_and_fusion, f32[1024,4096]{1,0:T(8,128)} %fusion.44, ...), kind=kOutput, calls=%fused_computation.12 | convolution fusion | flops 592441344 | bytes 69881856 | tf_op jit(solution)/shard_map/dot_general | solution.py:79
  240.5 20.8 %fusion.3 = (f32[1024]{0:T(1024)S(1)}, f32[1024]{0:T(1024)S(1)}, f32[1024]{0:T(1024)S(1)}) fusion(f32[1024,4096]{1,0:T(8,128)} %fusion.50, f32[1024]{0:T(1024)S(1)} %get-tuple-element.5, pred[128,4096]{1,0:T(8,128)(4,1)} %compare_and_fusion, f32[1024]{0:T(1024)S(1)} %get-tuple-element.4, f32[1024,4096]{1,0:T(8,128)} %fusion.44, ...), kind=kLoop, calls=%fused_computation.14 | loop fusion | flops 50328576 | bytes 50880512 | tf_op jit(solution)/shard_map/reduce_sum | solution.py:87
  263.5 9.8 %fusion.62 = bf16[128,8,64]{2,1,0:T(8,128)(2,1)} fusion(bf16[2048,256]{1,0:T(8,128)(2,1)} %get-tuple-element.12, bf16[2048,256]{1,0:T(8,128)(2,1)} %bitcast.223, f32[1024,4096]{1,0:T(8,128)} %get-tuple-element.25, f32[1024]{0:T(1024)S(1)} %get-tuple-element.3, pred[128,4096]{1,0:T(8,128)(4,1)S(1)} %copy-done.3, f32[128,8]{1,0:T(8,128)S(1)} %div.68), kind=kOutput, calls=%fused_computation.84 | convolution fusion | flops 554827776 | bytes 19537920 | tf_op jit(solution)/shard_map/dot_general | solution.py:88
  273.3 9.2 %fusion.72 = bf16[128,8,64]{2,1,0:T(8,128)(2,1)} fusion(bf16[2048,256]{1,0:T(8,128)(2,1)} %bitcast.224, bf16[2048,256]{1,0:T(8,128)(2,1)} %get-tuple-element.12, f32[1024,4096]{1,0:T(8,128)} %fusion.44, f32[1024]{0:T(1024)S(1)} %get-tuple-element.4, pred[128,4096]{1,0:T(8,128)(4,1)S(1)} %copy-done.3, f32[128,8]{1,0:T(8,128)} %div.65), kind=kOutput, calls=%fused_computation.86 | convolution fusion | flops 554827776 | bytes 19537920 | tf_op jit(solution)/shard_map/dot_general | solution.py:88
  282.5 6.5 %fusion.82 = bf16[128,8,64]{2,1,0:T(8,128)(2,1)} fusion(bf16[2048,256]{1,0:T(8,128)(2,1)} %bitcast.225, bf16[2048,256]{1,0:T(8,128)(2,1)} %get-tuple-element.12, f32[1024,4096]{1,0:T(8,128)S(1)} %bitcast.207, f32[1024]{0:T(1024)S(1)} %get-tuple-element.5, pred[128,4096]{1,0:T(8,128)(4,1)S(1)} %copy-done.3, f32[128,8]{1,0:T(8,128)} %div.62), kind=kOutput, calls=%fused_computation.88 | convolution fusion | flops 554827776 | bytes 19537920 | tf_op jit(solution)/shard_map/dot_general | solution.py:88
  289.0 8.8 %fusion.92 = bf16[128,8,64]{2,1,0:T(8,128)(2,1)S(1)} fusion(bf16[2048,256]{1,0:T(8,128)(2,1)} %bitcast.226, bf16[2048,256]{1,0:T(8,128)(2,1)} %get-tuple-element.12, f32[1024,4096]{1,0:T(8,128)} %get-tuple-element.24, f32[1024]{0:T(1024)S(1)} %get-tuple-element.23, pred[128,4096]{1,0:T(8,128)(4,1)S(1)} %copy-done.3, f32[128,8]{1,0:T(8,128)} %div.59), kind=kOutput, calls=%fused_computation.90 | convolution fusion | flops 554827776 | bytes 19537920 | tf_op jit(solution)/shard_map/dot_general | solution.py:88
  298.1 1.9 copy.81
  300.0 4.9 multiply_reduce_fusion
  306.0 13.7 %collective-permute-done = bf16[128,2048]{1,0:T(8,128)(2,1)S(1)} collective-permute-done((bf16[128,2048]{1,0:T(8,128)(2,1)S(1)}, bf16[128,2048]{1,0:T(8,128)(2,1)S(1)}, u32[]{:S(2)}, u32[]{:S(2)}) %collective-permute-start) | collective-permute-done | bytes 524320 | tf_op jit(solution)/shard_map/ppermute | solution.py:30
  320.6 5.3 collective-permute-start.8
  325.9 8.4 %collective-permute-done.1 = bf16[128,2048]{1,0:T(8,128)(2,1)S(1)} collective-permute-done((bf16[128,2048]{1,0:T(8,128)(2,1)S(1)}, bf16[128,2048]{1,0:T(8,128)(2,1)S(1)}, u32[]{:S(2)}, u32[]{:S(2)}) %collective-permute-start.1) | collective-permute-done | bytes 524320 | tf_op jit(solution)/shard_map/ppermute | solution.py:30
  335.2 5.3 collective-permute-start.9
  340.5 6.7 %collective-permute-done.2 = bf16[128,2048]{1,0:T(8,128)(2,1)S(1)} collective-permute-done((bf16[128,2048]{1,0:T(8,128)(2,1)S(1)}, bf16[128,2048]{1,0:T(8,128)(2,1)S(1)}, u32[]{:S(2)}, u32[]{:S(2)}) %collective-permute-start.2) | collective-permute-done | bytes 524320 | tf_op jit(solution)/shard_map/ppermute | solution.py:30
  347.2 5.8 %collective-permute-start.10 = (bf16[128,2048]{1,0:T(8,128)(2,1)S(1)}, bf16[128,2048]{1,0:T(8,128)(2,1)S(1)}, u32[]{:S(2)}, u32[]{:S(2)}) collective-permute-start(bf16[128,2048]{1,0:T(8,128)(2,1)S(1)} %collective-permute-done.9), channel_id=1, source_target_pairs={{1,0},{2,1},{3,2},{4,3},{5,4},{6,5},{7,6},{8,7},{9,8},{10,9},{11,1... | collective-permute-start | bytes 1572872 | tf_op jit(solution)/shard_map/ppermute | solution.py:32
  353.0 7.0 %collective-permute-done.3 = bf16[128,2048]{1,0:T(8,128)(2,1)S(1)} collective-permute-done((bf16[128,2048]{1,0:T(8,128)(2,1)S(1)}, bf16[128,2048]{1,0:T(8,128)(2,1)S(1)}, u32[]{:S(2)}, u32[]{:S(2)}) %collective-permute-start.3) | collective-permute-done | bytes 524320 | tf_op jit(solution)/shard_map/ppermute | solution.py:30
  360.4 5.8 %collective-permute-start.11 = (bf16[128,2048]{1,0:T(8,128)(2,1)S(1)}, bf16[128,2048]{1,0:T(8,128)(2,1)S(1)}, u32[]{:S(2)}, u32[]{:S(2)}) collective-permute-start(bf16[128,2048]{1,0:T(8,128)(2,1)S(1)} %collective-permute-done.10), channel_id=1, source_target_pairs={{1,0},{2,1},{3,2},{4,3},{5,4},{6,5},{7,6},{8,7},{9,8},{10,9},{11,1... | collective-permute-start | bytes 1572872 | tf_op jit(solution)/shard_map/ppermute | solution.py:32
  366.2 7.9 %collective-permute-done.4 = bf16[128,2048]{1,0:T(8,128)(2,1)S(1)} collective-permute-done((bf16[128,2048]{1,0:T(8,128)(2,1)S(1)}, bf16[128,2048]{1,0:T(8,128)(2,1)S(1)}, u32[]{:S(2)}, u32[]{:S(2)}) %collective-permute-start.4) | collective-permute-done | bytes 524320 | tf_op jit(solution)/shard_map/ppermute | solution.py:30
  374.9 5.6 collective-permute-start.12
  380.5 8.8 %collective-permute-done.5 = bf16[128,2048]{1,0:T(8,128)(2,1)S(1)} collective-permute-done((bf16[128,2048]{1,0:T(8,128)(2,1)S(1)}, bf16[128,2048]{1,0:T(8,128)(2,1)S(1)}, u32[]{:S(2)}, u32[]{:S(2)}) %collective-permute-start.5) | collective-permute-done | bytes 524320 | tf_op jit(solution)/shard_map/ppermute | solution.py:30
  389.8 5.9 %collective-permute-start.13 = (bf16[128,2048]{1,0:T(8,128)(2,1)}, bf16[128,2048]{1,0:T(8,128)(2,1)}, u32[]{:S(2)}, u32[]{:S(2)}) collective-permute-start(bf16[128,2048]{1,0:T(8,128)(2,1)} %collective-permute-done.12), channel_id=1, source_target_pairs={{1,0},{2,1},{3,2},{4,3},{5,4},{6,5},{7,6},{8,7},{9,8},{10,9},{11,1... | collective-permute-start | bytes 1572872 | tf_op jit(solution)/shard_map/ppermute | solution.py:32
  395.7 9.6 %collective-permute-done.6 = bf16[128,2048]{1,0:T(8,128)(2,1)} collective-permute-done((bf16[128,2048]{1,0:T(8,128)(2,1)S(1)}, bf16[128,2048]{1,0:T(8,128)(2,1)}, u32[]{:S(2)}, u32[]{:S(2)}) %collective-permute-start.6) | collective-permute-done | bytes 524320 | tf_op jit(solution)/shard_map/ppermute | solution.py:30
  405.4 1.1 collective-permute-done.13
  406.5 5.8 %collective-permute-start.14 = (bf16[128,2048]{1,0:T(8,128)(2,1)}, bf16[128,2048]{1,0:T(8,128)(2,1)S(1)}, u32[]{:S(2)}, u32[]{:S(2)}) collective-permute-start(bf16[128,2048]{1,0:T(8,128)(2,1)} %collective-permute-done.13), channel_id=1, source_target_pairs={{1,0},{2,1},{3,2},{4,3},{5,4},{6,5},{7,6},{8,7},{9,8},{10,9},{11,1... | collective-permute-start | bytes 1572872 | tf_op jit(solution)/shard_map/ppermute | solution.py:32
  412.3 5.8 %collective-permute-done.7 = bf16[128,2048]{1,0:T(8,128)(2,1)} collective-permute-done((bf16[128,2048]{1,0:T(8,128)(2,1)}, bf16[128,2048]{1,0:T(8,128)(2,1)}, u32[]{:S(2)}, u32[]{:S(2)}) %collective-permute-start.7) | collective-permute-done | bytes 524320 | tf_op jit(solution)/shard_map/ppermute | solution.py:30
  418.2 1.9 bitcast_dynamic-update-slice_fusion.15
  420.0 1.9 bitcast_dynamic-update-slice_fusion.14
  422.0 1.9 bitcast_dynamic-update-slice_fusion.13
  423.9 1.9 bitcast_dynamic-update-slice_fusion.12
  425.7 1.9 bitcast_dynamic-update-slice_fusion.11
  427.6 1.9 bitcast_dynamic-update-slice_fusion.10
  429.5 1.9 bitcast_dynamic-update-slice_fusion.9
  431.4 1.9 bitcast_dynamic-update-slice_fusion.8
  433.3 0.9 bitcast_dynamic-update-slice_fusion.7
  437.7 1.9 bitcast_dynamic-update-slice_fusion.2
  439.6 1.9 bitcast_dynamic-update-slice_fusion.1
  442.4 8.3 %gather_fusion.1 = bf16[16,128,2048]{2,1,0:T(8,128)(2,1)} fusion(bf16[16,128,2048]{2,1,0:T(8,128)(2,1)} %bitcast_dynamic-update-slice_fusion, s32[1024]{0:T(1024)S(1)} %pad_clamp_fusion), kind=kCustom, calls=%fused_computation.1 | custom fusion | bytes 16777280 | tf_op jit(solution)/shard_map/gather | solution.py:35
  450.8 10.5 %fusion.130 = f32[2048,512]{1,0:T(8,128)} fusion(bf16[2048,2048]{1,0:T(8,128)(2,1)} %bitcast.212, bf16[2048,512]{1,0:T(8,128)(2,1)} %param.17), kind=kOutput, calls=%fused_computation.167 | convolution fusion | flops 4294967296 | bytes 14680064 | tf_op jit(solution)/shard_map/dot_general | solution.py:167
  461.2 14.7 %convolution_convert_fusion.1 = bf16[2048,2048]{1,0:T(8,128)(2,1)} fusion(bf16[512,2048]{1,0:T(8,128)(2,1)S(1)} %copy-done, f32[2048,512]{1,0:T(8,128)} %fusion.130, bf16[2048,2048]{1,0:T(8,128)(2,1)} %bitcast.213, bf16[2048,512]{1,0:T(8,128)(2,1)} %param.18), kind=kOutput, calls=%fused_computation.36 | convolution fusion | flops 8600420352 | bytes 25165824 | tf_op jit(solution)/shard_map/dot_general | solution.py:171
  476.0 1.0 copy-done.6
  477.0 1.0 reshape_squeeze.3
  478.1 1.7 copy.82
  479.9 1.2 copy.91
  482.6 75.8 %reduce-scatter.2.cloned.1.call-done = bf16[128,2048]{1,0:T(8,128)(2,1)} async-done(((bf16[2048,2048]{1,0:T(8,128)(2,1)}), bf16[128,2048]{1,0:T(8,128)(2,1)}) %reduce-scatter.2.cloned.1.call-update) | async-done | bytes 524304 | tf_op jit(solution)/shard_map/reduce_scatter | solution.py:170
  558.4 1.9 fusion.97
  (131 shorter events, 23.5 us)
Async XLA Ops:
  7.2 454.1 %copy-start = (bf16[512,2048]{1,0:T(8,128)(2,1)S(1)}, bf16[512,2048]{1,0:T(8,128)(2,1)}, u32[]{:S(2)}) copy-start(bf16[512,2048]{1,0:T(8,128)(2,1)} %param.19) | copy-start | bytes 6291460
  7.2 63.4 %all-gather.6.cloned.1.call-start = ((), (), s32[]{:S(2)}) async-start(), calls=%async_computation.1 | async-start | bytes 11796480 | tf_op jit(solution)/shard_map/all_gather | solution.py:120
  7.9 126.7 %all-gather.12.cloned.1.call-start = ((), (), s32[]{:S(2)}) async-start(), calls=%async_computation.5 | async-start | bytes 6684672 | tf_op jit(solution)/shard_map/all_gather | solution.py:151
  8.7 172.8 %all-gather.8.cloned.1.call-start = ((), (), s32[]{:S(2)}) async-start(), calls=%async_computation.2 | async-start | bytes 2228224 | tf_op jit(solution)/shard_map/all_gather | solution.py:152
  78.4 61.0 %copy-start.4 = (f32[128,2560]{1,0:T(8,128)}, f32[128,2560]{1,0:T(8,128)S(1)}, u32[]{:S(2)}) copy-start(f32[128,2560]{1,0:T(8,128)S(1)} %fusion.98) | copy-start | bytes 3932164
  81.7 65.3 %copy-start.25 = (f32[128,32]{0,1:T(8,128)S(1)}, f32[128,32]{0,1:T(8,128)}, u32[]{:S(2)}) copy-start(f32[128,32]{0,1:T(8,128)} %get-tuple-element.22) | copy-start | bytes 49156
  81.7 218.3 %all-gather.10.cloned.1.call-start = ((), (), s32[]{:S(2)}) async-start(), calls=%async_computation.3 | async-start | bytes 9437184 | tf_op jit(solution)/shard_map/all_gather | solution.py:161
  82.3 476.1 %reduce-scatter.2.cloned.1.call-start = ((), (), s32[]{:S(2)}) async-start(), calls=%async_computation.4 | async-start | bytes 8912896 | tf_op jit(solution)/shard_map/reduce_scatter | solution.py:170
  184.2 18.6 %copy-start.1 = (bf16[2048,256]{1,0:T(8,128)(2,1)}, bf16[2048,256]{1,0:T(8,128)(2,1)S(1)}, u32[]{:S(2)}) copy-start(bf16[2048,256]{1,0:T(8,128)(2,1)S(1)} %get-tuple-element.11) | copy-start | bytes 3145732
  184.2 10.5 %copy-start.7 = (bf16[1024,64]{1,0:T(8,128)(2,1)S(1)}, bf16[1024,64]{1,0:T(8,128)(2,1)}, u32[]{:S(2)}) copy-start(bf16[1024,64]{1,0:T(8,128)(2,1)} %reshape.360) | copy-start | bytes 393220
  194.6 8.2 %copy-start.2 = (pred[128,4096]{1,0:T(8,128)(4,1)S(1)}, pred[128,4096]{1,0:T(8,128)(4,1)}, u32[]{:S(2)}) copy-start(pred[128,4096]{1,0:T(8,128)(4,1)} %compare_and_fusion) | copy-start | bytes 1572868
  240.5 23.1 %copy-start.3 = (pred[128,4096]{1,0:T(8,128)(4,1)S(1)}, pred[128,4096]{1,0:T(8,128)(4,1)}, u32[]{:S(2)}) copy-start(pred[128,4096]{1,0:T(8,128)(4,1)} %compare_and_fusion) | copy-start | bytes 1572868
  263.5 19.0 %slice-start = ((s8[16777216]{0:T(1024)(128)(4,1)}), s8[4194304]{0:T(1024)(128)(4,1)S(1)}, s32[]{:S(2)}) async-start(s8[16777216]{0:T(1024)(128)(4,1)} %bitcast.206), calls=%async_computation.6 | async-start | bytes 8388608
  263.5 19.0 %slice-start.1 = ((s8[16777216]{0:T(1024)(128)(4,1)}), s8[4194304]{0:T(1024)(128)(4,1)S(1)}, s32[]{:S(2)}) async-start(s8[16777216]{0:T(1024)(128)(4,1)} %bitcast.206), calls=%async_computation.7 | async-start | bytes 8388608
  273.3 9.2 %slice-start.2 = ((s8[16777216]{0:T(1024)(128)(4,1)}), s8[4194304]{0:T(1024)(128)(4,1)S(1)}, s32[]{:S(2)}) async-start(s8[16777216]{0:T(1024)(128)(4,1)} %bitcast.206), calls=%async_computation.8 | async-start | bytes 8388608
  273.3 9.2 %slice-start.3 = ((s8[16777216]{0:T(1024)(128)(4,1)}), s8[4194304]{0:T(1024)(128)(4,1)S(1)}, s32[]{:S(2)}) async-start(s8[16777216]{0:T(1024)(128)(4,1)} %bitcast.206), calls=%async_computation.9 | async-start | bytes 8388608
  289.0 8.8 %copy-start.22 = (bf16[128,8,64]{2,1,0:T(8,128)(2,1)S(1)}, bf16[128,8,64]{2,1,0:T(8,128)(2,1)}, u32[]{:S(2)}) copy-start(bf16[128,8,64]{2,1,0:T(8,128)(2,1)} %fusion.62) | copy-start | bytes 393220
  289.0 8.8 %copy-start.23 = (bf16[128,8,64]{2,1,0:T(8,128)(2,1)S(1)}, bf16[128,8,64]{2,1,0:T(8,128)(2,1)}, u32[]{:S(2)}) copy-start(bf16[128,8,64]{2,1,0:T(8,128)(2,1)} %fusion.72) | copy-start | bytes 393220
  289.0 8.8 %copy-start.24 = (bf16[128,8,64]{2,1,0:T(8,128)(2,1)S(1)}, bf16[128,8,64]{2,1,0:T(8,128)(2,1)}, u32[]{:S(2)}) copy-start(bf16[128,8,64]{2,1,0:T(8,128)(2,1)} %fusion.82) | copy-start | bytes 393220
  300.0 5.0 copy-start.26
  305.1 14.6 %collective-permute-start = (bf16[128,2048]{1,0:T(8,128)(2,1)S(1)}, bf16[128,2048]{1,0:T(8,128)(2,1)S(1)}, u32[]{:S(2)}, u32[]{:S(2)}) collective-permute-start(bf16[128,2048]{1,0:T(8,128)(2,1)S(1)} %multiply_convert_fusion.1), channel_id=1, source_target_pairs={{0,1},{1,2},{2,3},{3,4},{4,5},{5,6},{6,7},{7,8},{8,9},{9,10},{10,1... | collective-permute-start | bytes 1572872 | tf_op jit(solution)/shard_map/ppermute | solution.py:30
  319.8 0.8 copy-start.8
  320.6 13.7 %collective-permute-start.1 = (bf16[128,2048]{1,0:T(8,128)(2,1)S(1)}, bf16[128,2048]{1,0:T(8,128)(2,1)S(1)}, u32[]{:S(2)}, u32[]{:S(2)}) collective-permute-start(bf16[128,2048]{1,0:T(8,128)(2,1)S(1)} %collective-permute-done), channel_id=1, source_target_pairs={{0,1},{1,2},{2,3},{3,4},{4,5},{5,6},{6,7},{7,8},{8,9},{9,10},{10,1... | collective-permute-start | bytes 1572872 | tf_op jit(solution)/shard_map/ppermute | solution.py:30
  320.6 13.7 %collective-permute-start.8 = (bf16[128,2048]{1,0:T(8,128)(2,1)S(1)}, bf16[128,2048]{1,0:T(8,128)(2,1)S(1)}, u32[]{:S(2)}, u32[]{:S(2)}) collective-permute-start(bf16[128,2048]{1,0:T(8,128)(2,1)S(1)} %multiply_convert_fusion.1), channel_id=1, source_target_pairs={{1,0},{2,1},{3,2},{4,3},{5,4},{6,5},{7,6},{8,7},{9,8},{10,9},{11,1... | collective-permute-start | bytes 1572872 | tf_op jit(solution)/shard_map/ppermute | solution.py:32
  334.3 12.9 %copy-start.11 = (bf16[128,2048]{1,0:T(8,128)(2,1)}, bf16[128,2048]{1,0:T(8,128)(2,1)S(1)}, u32[]{:S(2)}) copy-start(bf16[128,2048]{1,0:T(8,128)(2,1)S(1)} %collective-permute-done.1) | copy-start | bytes 1572868
  334.3 12.9 %collective-permute-start.2 = (bf16[128,2048]{1,0:T(8,128)(2,1)S(1)}, bf16[128,2048]{1,0:T(8,128)(2,1)S(1)}, u32[]{:S(2)}, u32[]{:S(2)}) collective-permute-start(bf16[128,2048]{1,0:T(8,128)(2,1)S(1)} %collective-permute-done.1), channel_id=1, source_target_pairs={{0,1},{1,2},{2,3},{3,4},{4,5},{5,6},{6,7},{7,8},{8,9},{9,10},{10,1... | collective-permute-start | bytes 1572872 | tf_op jit(solution)/shard_map/ppermute | solution.py:30
  334.3 0.8 copy-start.9
  335.2 12.1 %collective-permute-start.9 = (bf16[128,2048]{1,0:T(8,128)(2,1)S(1)}, bf16[128,2048]{1,0:T(8,128)(2,1)S(1)}, u32[]{:S(2)}, u32[]{:S(2)}) collective-permute-start(bf16[128,2048]{1,0:T(8,128)(2,1)S(1)} %collective-permute-done.8), channel_id=1, source_target_pairs={{1,0},{2,1},{3,2},{4,3},{5,4},{6,5},{7,6},{8,7},{9,8},{10,9},{11,1... | collective-permute-start | bytes 1572872 | tf_op jit(solution)/shard_map/ppermute | solution.py:32
  347.2 13.2 %copy-start.14 = (bf16[128,2048]{1,0:T(8,128)(2,1)}, bf16[128,2048]{1,0:T(8,128)(2,1)S(1)}, u32[]{:S(2)}) copy-start(bf16[128,2048]{1,0:T(8,128)(2,1)S(1)} %collective-permute-done.2) | copy-start | bytes 1572868
  347.2 12.9 %collective-permute-start.3 = (bf16[128,2048]{1,0:T(8,128)(2,1)S(1)}, bf16[128,2048]{1,0:T(8,128)(2,1)S(1)}, u32[]{:S(2)}, u32[]{:S(2)}) collective-permute-start(bf16[128,2048]{1,0:T(8,128)(2,1)S(1)} %collective-permute-done.2), channel_id=1, source_target_pairs={{0,1},{1,2},{2,3},{3,4},{4,5},{5,6},{6,7},{7,8},{8,9},{9,10},{10,1... | collective-permute-start | bytes 1572872 | tf_op jit(solution)/shard_map/ppermute | solution.py:30
  347.2 5.8 %copy-start.12 = (bf16[128,2048]{1,0:T(8,128)(2,1)}, bf16[128,2048]{1,0:T(8,128)(2,1)S(1)}, u32[]{:S(2)}) copy-start(bf16[128,2048]{1,0:T(8,128)(2,1)S(1)} %collective-permute-done.9) | copy-start | bytes 1572868
  347.2 13.1 %collective-permute-start.10 = (bf16[128,2048]{1,0:T(8,128)(2,1)S(1)}, bf16[128,2048]{1,0:T(8,128)(2,1)S(1)}, u32[]{:S(2)}, u32[]{:S(2)}) collective-permute-start(bf16[128,2048]{1,0:T(8,128)(2,1)S(1)} %collective-permute-done.9), channel_id=1, source_target_pairs={{1,0},{2,1},{3,2},{4,3},{5,4},{6,5},{7,6},{8,7},{9,8},{10,9},{11,1... | collective-permute-start | bytes 1572872 | tf_op jit(solution)/shard_map/ppermute | solution.py:32
  360.1 29.8 %copy-start.19 = (bf16[128,2048]{1,0:T(8,128)(2,1)}, bf16[128,2048]{1,0:T(8,128)(2,1)S(1)}, u32[]{:S(2)}) copy-start(bf16[128,2048]{1,0:T(8,128)(2,1)S(1)} %collective-permute-done.3) | copy-start | bytes 1572868
  360.1 14.0 %collective-permute-start.4 = (bf16[128,2048]{1,0:T(8,128)(2,1)S(1)}, bf16[128,2048]{1,0:T(8,128)(2,1)S(1)}, u32[]{:S(2)}, u32[]{:S(2)}) collective-permute-start(bf16[128,2048]{1,0:T(8,128)(2,1)S(1)} %collective-permute-done.3), channel_id=1, source_target_pairs={{0,1},{1,2},{2,3},{3,4},{4,5},{5,6},{6,7},{7,8},{8,9},{9,10},{10,1... | collective-permute-start | bytes 1572872 | tf_op jit(solution)/shard_map/ppermute | solution.py:30
  360.4 5.8 %copy-start.15 = (bf16[128,2048]{1,0:T(8,128)(2,1)}, bf16[128,2048]{1,0:T(8,128)(2,1)S(1)}, u32[]{:S(2)}) copy-start(bf16[128,2048]{1,0:T(8,128)(2,1)S(1)} %collective-permute-done.10) | copy-start | bytes 1572868
  360.4 13.7 %collective-permute-start.11 = (bf16[128,2048]{1,0:T(8,128)(2,1)S(1)}, bf16[128,2048]{1,0:T(8,128)(2,1)S(1)}, u32[]{:S(2)}, u32[]{:S(2)}) collective-permute-start(bf16[128,2048]{1,0:T(8,128)(2,1)S(1)} %collective-permute-done.10), channel_id=1, source_target_pairs={{1,0},{2,1},{3,2},{4,3},{5,4},{6,5},{7,6},{8,7},{9,8},{10,9},{11,1... | collective-permute-start | bytes 1572872 | tf_op jit(solution)/shard_map/ppermute | solution.py:32
  374.1 21.7 %copy-start.20 = (bf16[128,2048]{1,0:T(8,128)(2,1)}, bf16[128,2048]{1,0:T(8,128)(2,1)S(1)}, u32[]{:S(2)}) copy-start(bf16[128,2048]{1,0:T(8,128)(2,1)S(1)} %collective-permute-done.4) | copy-start | bytes 1572868
  374.1 15.2 %collective-permute-start.5 = (bf16[128,2048]{1,0:T(8,128)(2,1)S(1)}, bf16[128,2048]{1,0:T(8,128)(2,1)S(1)}, u32[]{:S(2)}, u32[]{:S(2)}) collective-permute-start(bf16[128,2048]{1,0:T(8,128)(2,1)S(1)} %collective-permute-done.4), channel_id=1, source_target_pairs={{0,1},{1,2},{2,3},{3,4},{4,5},{5,6},{6,7},{7,8},{8,9},{9,10},{10,1... | collective-permute-start | bytes 1572872 | tf_op jit(solution)/shard_map/ppermute | solution.py:30
  374.1 0.8 copy-start.17
  374.9 14.9 %collective-permute-start.12 = (bf16[128,2048]{1,0:T(8,128)(2,1)S(1)}, bf16[128,2048]{1,0:T(8,128)(2,1)}, u32[]{:S(2)}, u32[]{:S(2)}) collective-permute-start(bf16[128,2048]{1,0:T(8,128)(2,1)S(1)} %collective-permute-done.11), channel_id=1, source_target_pairs={{1,0},{2,1},{3,2},{4,3},{5,4},{6,5},{7,6},{8,7},{9,8},{10,9},{11,1... | collective-permute-start | bytes 1572872 | tf_op jit(solution)/shard_map/ppermute | solution.py:32
  389.2 16.1 %copy-start.21 = (bf16[128,2048]{1,0:T(8,128)(2,1)}, bf16[128,2048]{1,0:T(8,128)(2,1)S(1)}, u32[]{:S(2)}) copy-start(bf16[128,2048]{1,0:T(8,128)(2,1)S(1)} %collective-permute-done.5) | copy-start | bytes 1572868
  389.2 16.1 %collective-permute-start.6 = (bf16[128,2048]{1,0:T(8,128)(2,1)S(1)}, bf16[128,2048]{1,0:T(8,128)(2,1)}, u32[]{:S(2)}, u32[]{:S(2)}) collective-permute-start(bf16[128,2048]{1,0:T(8,128)(2,1)S(1)} %collective-permute-done.5), channel_id=1, source_target_pairs={{0,1},{1,2},{2,3},{3,4},{4,5},{5,6},{6,7},{7,8},{8,9},{9,10},{10,1... | collective-permute-start | bytes 1572872 | tf_op jit(solution)/shard_map/ppermute | solution.py:30
  389.8 16.7 %collective-permute-start.13 = (bf16[128,2048]{1,0:T(8,128)(2,1)}, bf16[128,2048]{1,0:T(8,128)(2,1)}, u32[]{:S(2)}, u32[]{:S(2)}) collective-permute-start(bf16[128,2048]{1,0:T(8,128)(2,1)} %collective-permute-done.12), channel_id=1, source_target_pairs={{1,0},{2,1},{3,2},{4,3},{5,4},{6,5},{7,6},{8,7},{9,8},{10,9},{11,1... | collective-permute-start | bytes 1572872 | tf_op jit(solution)/shard_map/ppermute | solution.py:32
  405.4 12.8 %collective-permute-start.7 = (bf16[128,2048]{1,0:T(8,128)(2,1)}, bf16[128,2048]{1,0:T(8,128)(2,1)}, u32[]{:S(2)}, u32[]{:S(2)}) collective-permute-start(bf16[128,2048]{1,0:T(8,128)(2,1)} %collective-permute-done.6), channel_id=1, source_target_pairs={{0,1},{1,2},{2,3},{3,4},{4,5},{5,6},{6,7},{7,8},{8,9},{9,10},{10,1... | collective-permute-start | bytes 1572872 | tf_op jit(solution)/shard_map/ppermute | solution.py:30
  405.4 28.9 %copy-start.10 = (bf16[128,2048]{1,0:T(8,128)(2,1)S(1)}, bf16[128,2048]{1,0:T(8,128)(2,1)}, u32[]{:S(2)}) copy-start(bf16[128,2048]{1,0:T(8,128)(2,1)} %copy-done.9) | copy-start | bytes 1572868
  405.4 29.8 %copy-start.13 = (bf16[128,2048]{1,0:T(8,128)(2,1)S(1)}, bf16[128,2048]{1,0:T(8,128)(2,1)}, u32[]{:S(2)}) copy-start(bf16[128,2048]{1,0:T(8,128)(2,1)} %copy-done.12) | copy-start | bytes 1572868
  405.4 30.6 %copy-start.16 = (bf16[128,2048]{1,0:T(8,128)(2,1)S(1)}, bf16[128,2048]{1,0:T(8,128)(2,1)}, u32[]{:S(2)}) copy-start(bf16[128,2048]{1,0:T(8,128)(2,1)} %copy-done.15) | copy-start | bytes 1572868
  405.4 31.5 %copy-start.18 = (bf16[128,2048]{1,0:T(8,128)(2,1)S(1)}, bf16[128,2048]{1,0:T(8,128)(2,1)}, u32[]{:S(2)}) copy-start(bf16[128,2048]{1,0:T(8,128)(2,1)} %copy-done.17) | copy-start | bytes 1572868
  406.5 35.0 %collective-permute-start.14 = (bf16[128,2048]{1,0:T(8,128)(2,1)}, bf16[128,2048]{1,0:T(8,128)(2,1)S(1)}, u32[]{:S(2)}, u32[]{:S(2)}) collective-permute-start(bf16[128,2048]{1,0:T(8,128)(2,1)} %collective-permute-done.13), channel_id=1, source_target_pairs={{1,0},{2,1},{3,2},{4,3},{5,4},{6,5},{7,6},{8,7},{9,8},{10,9},{11,1... | collective-permute-start | bytes 1572872 | tf_op jit(solution)/shard_map/ppermute | solution.py:32
  476.0 1.0 copy-start.6
  476.0 2.0 copy-start.27
  477.9 3.1 copy-start.5
Sparse Core Ops, SparseCore 0:
  9.7 60.9 all-gather.5
  72.8 61.7 all-gather.11
  136.8 44.6 all-gather.7
  183.0 48.8 all-gather.9
  476.1 82.1 reduce-scatter.1
